TPU v7x, 512 devices: a whole 4x4x16 slice. The times are simulated.
512 devices in a mesh: dp: 8 (over z_hi, y), shard: 64 (over x, z_lo, core).
Axes of the slice: x: 4, y: 4, z: 16 (z_hi: 2, z_lo: 8; z = z_hi * 8 + z_lo), core: 2. Of those that a mesh axis runs over, the one named last changes fastest.
Arguments:
- context: bfloat16 [8192, 4096], P('shard'), may hold values from -16 to 16
- projected: bfloat16 [8192, 4096], P('shard', 'dp'), may hold values from -6 to 6
- cotangent: bfloat16 [8192, 4096], P('shard', 'dp'), may hold values from -16 to 16
- modality: int32 [8192], P('shard'), may hold values from 0 to 2
- out_weight: bfloat16 [4096, 3, 4096], P('shard', None, 'dp'), may hold values from -0.09375 to 0.09375
- out_gain: float32 [3, 4096], P(None, 'dp'), may hold values from 0.25 to 1.75
Outputs:
- grad_context: bfloat16 [8192, 4096], P('shard', 'dp')
- grad_weight: float32 [4096, 3, 4096], P('shard', None, 'dp')
- grad_gain: float32 [3, 4096], P(None, 'dp')
All inputs are finite; a program needn't handle non-finite values.
Results may differ from a plain program's by a relative error of at most 0.0049.
Values may be sent and summed in bfloat16 or wider, within the bound.
No kernel may reach another device: no remote copies, remote signals or barrier semaphores. Data moves between devices by JAX's collectives and lax.ppermute only.
A program may use at most 64 MiB of HBM per device.

v0:
```python
import jax
import jax.numpy as jnp
from jax import lax
from jax.sharding import Mesh
from jax.sharding import PartitionSpec as P

D = 4096
DP = ("dp_0", "dp_1")
EPS = 1e-06


def from_everyone(shard, axis):
    count = lax.axis_size(axis)
    return lax.all_to_all(
        jnp.broadcast_to(shard[None], (count, *shard.shape)), axis, 0, 0, tiled=True
    )


def of_everyone(shard, axis):
    everything = from_everyone(shard, axis)
    return jnp.sum(everything, axis=0)


def packed_total(arrays, axis):
    ravelled, at, outs = (jnp.concatenate([a.reshape(-1) for a in arrays]), 0, [])
    total = of_everyone(ravelled, axis)
    for a in arrays:
        outs.append(total[at : at + a.size].reshape(a.shape))
        at += a.size
    return tuple(outs)


def sum_in_order(pieces, axes, order):
    lengths = [lax.axis_size(a) for a in axes]
    pieces = pieces.reshape(*lengths, *pieces.shape[1:])
    pieces = pieces.transpose(*order, *range(len(axes), pieces.ndim))
    pieces = pieces.reshape(-1, *pieces.shape[len(axes) :])
    for k in order:
        pieces = lax.psum_scatter(pieces, axes[k], scatter_dimension=0, tiled=True)
    return pieces[0]


def cut_along(shard, dim, count):
    lengths = shard.shape
    pieces = shard.reshape(*lengths[:dim], count, lengths[dim] // count, *lengths[dim + 1 :])
    return jnp.moveaxis(pieces, dim, 0)


def summed_rows(shard, axes, order, dim):
    count = lax.axis_size(axes)
    return sum_in_order(cut_along(shard, dim, count), axes, order)


def local(context, projected, cotangent, modality, out_weight, out_gain):
    towers = out_weight.shape[1]
    tower_ids = jnp.arange(towers, dtype=jnp.int32)
    onehot = (modality[:, None] == tower_ids[None, :]).astype(jnp.float32)
    proj_float = projected.astype(jnp.float32)
    cot_float = cotangent.astype(jnp.float32)
    gain_tok = jnp.dot(onehot, out_gain, precision=lax.Precision.HIGHEST)
    scaled = cot_float * gain_tok
    squares, raw_inner = packed_total(
        (
            jnp.sum(proj_float * proj_float, axis=1, keepdims=True),
            jnp.sum(scaled * proj_float, axis=1, keepdims=True),
        ),
        DP,
    )
    inverse_rms = lax.rsqrt(squares / D + EPS)
    normed = proj_float * inverse_rms
    inner = inverse_rms * raw_inner
    gain_terms = jnp.dot(onehot.T, cot_float * normed, precision=lax.Precision.HIGHEST)
    grad_gain = of_everyone(gain_terms, "shard")
    grad_proj = (inverse_rms * (scaled - normed * (inner / D))).astype(jnp.bfloat16)
    column_rows = lax.all_to_all(context, "shard", split_axis=1, concat_axis=0, tiled=True)
    row_count = out_weight.shape[0]
    piece_grad = lax.all_gather(grad_proj, "shard", axis=0, tiled=True)
    piece_ids = lax.all_gather(modality, "shard", axis=0, tiled=True)
    count = piece_grad.shape[0]
    piece_partial = jnp.zeros((count, row_count), jnp.float32)
    updated = []
    for member in range(towers):
        chosen = piece_ids[:, None] == member
        product = lax.dot_general(
            piece_grad,
            out_weight[:, member, :],
            (((1,), (1,)), ((), ())),
            preferred_element_type=jnp.float32,
        )
        piece_partial = piece_partial + chosen.astype(jnp.float32) * product
        masked = jnp.where(chosen, column_rows, jnp.zeros_like(column_rows))
        updated.append(
            lax.dot_general(
                masked, piece_grad, (((0,), (0,)), ((), ())), preferred_element_type=jnp.float32
            )
        )
    partial_value = piece_partial
    weight_accs, partial_value = (tuple(updated), partial_value)
    grad_weight = jnp.stack(weight_accs, axis=1)
    shard_count = lax.axis_size("shard")
    replica_count = lax.axis_size(DP)
    tok_here = grad_proj.shape[0]
    sub_rows = tok_here // replica_count
    grouped = partial_value.reshape(shard_count, replica_count, sub_rows, row_count)
    reduced = summed_rows(grouped, DP, (1, 0), 1).astype(jnp.bfloat16)
    reduced = reduced.reshape(shard_count, sub_rows, row_count)
    spread = lax.all_to_all(reduced, "shard", split_axis=0, concat_axis=2, tiled=True)
    settled = lax.all_to_all(spread, DP, split_axis=2, concat_axis=1, tiled=True)
    grad_context = settled.reshape(tok_here, settled.shape[2])
    return (grad_context, grad_weight, grad_gain)


def solution(mesh):
    finer = Mesh(mesh.devices.reshape(2, 4, mesh.shape["shard"]), ("dp_0", "dp_1", "shard"))
    return jax.shard_map(
        local,
        mesh=finer,
        in_specs=(
            P("shard", None),
            P("shard", DP),
            P("shard", DP),
            P("shard"),
            P("shard", None, DP),
            P(None, DP),
        ),
        out_specs=(P("shard", DP), P("shard", None, DP), P(None, DP)),
        check_vma=False,
    )
```

profile of v0, /device:TPU:32, one launch (start us, length us, event | category | flops | bytes accessed | tf_op | source)
XLA Modules:
  0.0 406.7 jit_solution(18081353275957798756)
XLA Ops:
  7.9 1.4 fusion.16
  9.3 31.5 %all_to_all.63 = f32[8,1,256]{2,1,0:T(1,128)S(1)} all-to-all(f32[8,1,256]{2,1,0:T(1,128)S(1)} %broadcast_in_dim.35), channel_id=1, replica_groups=mesh['dp_0'=2,'dp_1'=4,'shard'=64] {'dp_0','dp_1'}, dimensions={0} | all-to-all | bytes 16384 | tf_op jit(solution)/shard_map/all_to_all | solution.py:14
  40.9 1.7 fusion.14
  42.6 113.4 %all-gather = s32[64,1,128]{2,1,0:T(1,128)S(1)} all-gather(s32[1,1,128]{2,1,0:T(1,128)} %bitcast.89), channel_id=1, replica_groups=mesh['dp_0'=2,'dp_1'=4,'shard'=64] {'shard'}, dimensions={0}, use_global_device_ids=true | all-gather | bytes 33280 | tf_op jit(solution)/shard_map/all_gather | solution.py:78
  156.0 1.3 fusion.15
  157.3 0.9 broadcast_in_dim.39
  158.2 10.1 %all-to-all-start.4 = ((f32[64,3,512]{2,1,0:T(4,128)}), f32[64,3,512]{2,1,0:T(4,128)S(1)}, u32[]{:S(2)}, u32[]{:S(2)}) async-start(f32[64,3,512]{2,1,0:T(4,128)} %broadcast_in_dim.39), calls=%async_computation.6 | async-start | bytes 1048576 | tf_op jit(solution)/shard_map/all_to_all | solution.py:14
  168.3 6.2 %convolution_multiply_fusion = f32[8192,64]{0,1:T(8,128)S(1)} fusion(bf16[8192,512]{1,0:T(8,128)(2,1)} %all-gather.3.cloned.1.call-done, f32[8192]{0:T(1024)S(1)} %get-tuple-element.11, bf16[64,3,512]{2,0,1:T(8,128)(2,1)} %param.10), kind=kOutput, calls=%fused_computation | convolution fusion | flops 537395200 | bytes 10584064 | tf_op jit(solution)/shard_map/dot_general | solution.py:84
  174.5 2.6 convolution_multiply_fusion.1
  177.2 2.6 fusion.1
  179.8 2.7 copy.46
  182.5 4.5 %copy.47 = f32[2,4,64,1,16,64]{5,4,2,0,1,3:T(8,128)} copy(f32[2,4,64,1,16,64]{5,4,1,0,2,3:T(8,128)} %bitcast.81) | data formatting | bytes 4194304 | tf_op jit(solution)/shard_map/reshape | solution.py:35
  187.1 1.2 copy-done.2
  188.3 1.3 copy.52
  189.5 6.7 %all-to-all-done.4 = f32[64,3,512]{2,1,0:T(4,128)S(1)} async-done(((f32[64,3,512]{2,1,0:T(4,128)}), f32[64,3,512]{2,1,0:T(4,128)S(1)}, u32[]{:S(2)}, u32[]{:S(2)}) %all-to-all-start.4) | async-done | bytes 393248 | tf_op jit(solution)/shard_map/all_to_all | solution.py:14
  196.3 9.1 %all-to-all-start.3 = ((bf16[128,64,64]{0,2,1:T(8,128)(2,1)}), bf16[128,64,64]{0,2,1:T(8,128)(2,1)S(1)}, u32[]{:S(2)}, u32[]{:S(2)}) async-start(bf16[128,64,64]{0,2,1:T(8,128)(2,1)} %bitcast.20), calls=%async_computation.5 | async-start | bytes 2097152 | tf_op jit(solution)/shard_map/all_to_all | solution.py:75
  205.5 33.3 %reduce-scatter.3.cloned.1.call-done = f32[2,64,1,16,64]{4,3,1,0,2:T(8,128)} async-done(((f32[8,64,1,16,64]{4,3,1,0,2:T(8,128)}), f32[2,64,1,16,64]{4,3,1,0,2:T(8,128)}) %reduce-scatter.3.cloned.1.call-update) | async-done | bytes 524304 | tf_op jit(solution)/shard_map/reduce_scatter | solution.py:39
  239.5 15.5 %all-to-all-done.3 = bf16[128,64,64]{0,2,1:T(8,128)(2,1)S(1)} async-done(((bf16[128,64,64]{0,2,1:T(8,128)(2,1)}), bf16[128,64,64]{0,2,1:T(8,128)(2,1)S(1)}, u32[]{:S(2)}, u32[]{:S(2)}) %all-to-all-start.3) | async-done | bytes 1048608 | tf_op jit(solution)/shard_map/all_to_all | solution.py:75
  255.1 5.3 %convolution_bitcast_fusion = f32[64,1,512]{2,0,1:T(8,128)S(1)} fusion(bf16[8192,512]{1,0:T(8,128)(2,1)} %all-gather.3.cloned.1.call-done, pred[8192]{0:T(1024)(128)(4,1)S(1)} %get-tuple-element.12, bf16[128,64,64]{0,2,1:T(8,128)(2,1)S(1)} %all-to-all-done.3), kind=kOutput, calls=%fused_computation.6 | convolution fusion | flops 537395200 | bytes 9576448 | tf_op jit(solution)/shard_map/dot_general | solution.py:93
  260.3 46.1 %reduce-scatter.5.cloned.1.call-done = f32[1,64,1,16,64]{4,3,1,0,2:T(8,128)} async-done(((f32[2,64,1,16,64]{4,3,1,0,2:T(8,128)}), f32[1,64,1,16,64]{4,3,1,0,2:T(8,128)}) %reduce-scatter.5.cloned.1.call-update) | async-done | bytes 262160 | tf_op jit(solution)/shard_map/reduce_scatter | solution.py:39
  306.4 1.1 convert_bitcast_fusion
  308.3 14.9 %all-to-all-start.1 = ((bf16[64,2,512]{2,1,0:T(2,128)(2,1)}), bf16[64,2,512]{2,1,0:T(2,128)(2,1)S(1)}, u32[]{:S(2)}, u32[]{:S(2)}) async-start(bf16[64,2,512]{2,1,0:T(2,128)(2,1)} %reshape.65), calls=%async_computation.3 | async-start | bytes 262144 | tf_op jit(solution)/shard_map/all_to_all | solution.py:107
  323.2 4.9 %convolution_bitcast_fusion.1 = f32[64,1,512]{2,0,1:T(8,128)S(1)} fusion(bf16[8192,512]{1,0:T(8,128)(2,1)} %all-gather.3.cloned.1.call-done, pred[8192]{0:T(1024)(128)(4,1)S(1)} %get-tuple-element.14, bf16[128,64,64]{0,2,1:T(8,128)(2,1)S(1)} %all-to-all-done.3), kind=kOutput, calls=%fused_computation.7 | convolution fusion | flops 537395200 | bytes 9576448 | tf_op jit(solution)/shard_map/dot_general | solution.py:93
  328.1 8.7 %all-to-all-done.1 = bf16[64,2,512]{2,1,0:T(2,128)(2,1)S(1)} async-done(((bf16[64,2,512]{2,1,0:T(2,128)(2,1)}), bf16[64,2,512]{2,1,0:T(2,128)(2,1)S(1)}, u32[]{:S(2)}, u32[]{:S(2)}) %all-to-all-start.1) | async-done | bytes 131104 | tf_op jit(solution)/shard_map/all_to_all | solution.py:107
  337.4 2.7 copy.49
  340.7 23.5 %reduce.1 = bf16[4096,16]{1,0:T(8,128)(2,1)} reduce(bf16[4096,1,16]{2,1,0:T(2,128)(2,1)S(1)} %bitcast.82, bf16[]{:T(256)} %broadcast.57), dimensions={1}, to_apply=%bitcast.58.reduce_sub_computation | reduce | bytes 262146
  364.2 3.1 reshape.67
  367.3 10.1 %all-to-all-start.2 = ((bf16[8,2,4096]{2,1,0:T(2,128)(2,1)}), bf16[8,2,4096]{2,1,0:T(2,128)(2,1)S(1)}, u32[]{:S(2)}, u32[]{:S(2)}) async-start(bf16[8,2,4096]{2,1,0:T(2,128)(2,1)} %reshape.67), calls=%async_computation.4 | async-start | bytes 262144 | tf_op jit(solution)/shard_map/all_to_all | solution.py:108
  377.3 4.9 %convolution_bitcast_fusion.2 = f32[64,1,512]{2,0,1:T(8,128)S(1)} fusion(bf16[8192,512]{1,0:T(8,128)(2,1)} %all-gather.3.cloned.1.call-done, pred[8192]{0:T(1024)(128)(4,1)S(1)} %get-tuple-element.6, bf16[128,64,64]{0,2,1:T(8,128)(2,1)S(1)} %all-to-all-done.3), kind=kOutput, calls=%fused_computation.8 | convolution fusion | flops 537395200 | bytes 9576448 | tf_op jit(solution)/shard_map/dot_general | solution.py:93
  383.0 12.6 %all-to-all-done.2 = bf16[8,2,4096]{2,1,0:T(2,128)(2,1)S(1)} async-done(((bf16[8,2,4096]{2,1,0:T(2,128)(2,1)}), bf16[8,2,4096]{2,1,0:T(2,128)(2,1)S(1)}, u32[]{:S(2)}, u32[]{:S(2)}) %all-to-all-start.2) | async-done | bytes 131104 | tf_op jit(solution)/shard_map/all_to_all | solution.py:108
  395.6 1.8 reshape.68
  397.4 2.0 copy.50
  (29 shorter events, 5.1 us)
Async XLA Ops:
  7.2 0.7 copy-start
  7.2 161.1 %all-gather.3.cloned.1.call-start = ((), (), s32[]{:S(2)}) async-start(), calls=%async_computation.7 | async-start | bytes 8519680 | tf_op jit(solution)/shard_map/all_gather | solution.py:77
  158.2 38.1 %all-to-all-start.4 = ((f32[64,3,512]{2,1,0:T(4,128)}), f32[64,3,512]{2,1,0:T(4,128)S(1)}, u32[]{:S(2)}, u32[]{:S(2)}) async-start(f32[64,3,512]{2,1,0:T(4,128)} %broadcast_in_dim.39), calls=%async_computation.6 | async-start | bytes 1048576 | tf_op jit(solution)/shard_map/all_to_all | solution.py:14
  168.2 70.5 %reduce-scatter.3.cloned.1.call-start = ((), (), s32[]{:S(2)}) async-start(), calls=%async_computation.8 | async-start | bytes 5242880 | tf_op jit(solution)/shard_map/reduce_scatter | solution.py:39
  168.3 6.2 %copy-start.1 = (bf16[8192,512]{1,0:T(8,128)(2,1)S(1)}, bf16[8192,512]{1,0:T(8,128)(2,1)}, u32[]{:S(2)}) copy-start(bf16[8192,512]{1,0:T(8,128)(2,1)} %all-gather.3.cloned.1.call-done) | copy-start | bytes 25165828
  168.3 6.2 %copy-start.3 = (bf16[64,3,512]{2,0,1:T(8,128)(2,1)S(1)}, bf16[64,3,512]{2,0,1:T(8,128)(2,1)}, u32[]{:S(2)}) copy-start(bf16[64,3,512]{2,0,1:T(8,128)(2,1)} %param.10) | copy-start | bytes 589828
  187.0 1.2 copy-start.2
  196.3 58.8 %all-to-all-start.3 = ((bf16[128,64,64]{0,2,1:T(8,128)(2,1)}), bf16[128,64,64]{0,2,1:T(8,128)(2,1)S(1)}, u32[]{:S(2)}, u32[]{:S(2)}) async-start(bf16[128,64,64]{0,2,1:T(8,128)(2,1)} %bitcast.20), calls=%async_computation.5 | async-start | bytes 2097152 | tf_op jit(solution)/shard_map/all_to_all | solution.py:75
  205.4 101.0 %reduce-scatter.5.cloned.1.call-start = ((), (), s32[]{:S(2)}) async-start(), calls=%async_computation.9 | async-start | bytes 1572864 | tf_op jit(solution)/shard_map/reduce_scatter | solution.py:39
  308.3 28.5 %all-to-all-start.1 = ((bf16[64,2,512]{2,1,0:T(2,128)(2,1)}), bf16[64,2,512]{2,1,0:T(2,128)(2,1)S(1)}, u32[]{:S(2)}, u32[]{:S(2)}) async-start(bf16[64,2,512]{2,1,0:T(2,128)(2,1)} %reshape.65), calls=%async_computation.3 | async-start | bytes 262144 | tf_op jit(solution)/shard_map/all_to_all | solution.py:107
  367.3 28.3 %all-to-all-start.2 = ((bf16[8,2,4096]{2,1,0:T(2,128)(2,1)}), bf16[8,2,4096]{2,1,0:T(2,128)(2,1)S(1)}, u32[]{:S(2)}, u32[]{:S(2)}) async-start(bf16[8,2,4096]{2,1,0:T(2,128)(2,1)} %reshape.67), calls=%async_computation.4 | async-start | bytes 262144 | tf_op jit(solution)/shard_map/all_to_all | solution.py:108
Sparse Core Ops, SparseCore 0:
  42.7 119.8 all-gather.2
  187.2 51.5 reduce-scatter.2
  241.6 64.7 reduce-scatter.4
where the time goes:
time: 408 us; the launch traced here: 407 us
  blocking collectives  145 us (36%)
  waiting for transfers between devices  123 us (30%)
  starting transfers between devices  44.3 us (11%)
  matrix products  29.2 us (7%)
  other arithmetic  27.8 us (7%)
  local copies, waits for them, and re-layouts  23.6 us (6%)
  between operations  13.9 us (3%)
    all_gather x1, blocking collectives, local(): piece_ids = lax.all_gather(modality, 'shard', axis=0, tiled=True)  113 us
    reduce_scatter x2, waiting for transfers between devices, sum_in_order(): pieces = lax.psum_scatter(pieces, axes[k], scatter_dimension=0, tiled=True)  79.4 us
    all_to_all x1, blocking collectives, from_everyone(): lax.all_to_all(jnp.broadcast_to(shard[None], (count, *shard.shape)), axis...  31.5 us
    unnamed x1, other arithmetic  23.5 us
    all_to_all x1, waiting for transfers between devices, local(): lax.all_to_all(context, 'shard', split_axis=1, concat_axis=0, tiled=True)  15.5 us
    dot_general x3, matrix products, local(): lax.dot_general(masked, piece_grad, (((0,), (0,)), ((), ())), preferred_e...  15.1 us
    all_to_all x1, starting transfers between devices, local(): lax.all_to_all(reduced, 'shard', split_axis=0, concat_axis=2, tiled=True)  14.9 us
    all_to_all x1, waiting for transfers between devices, local(): lax.all_to_all(spread, DP, split_axis=2, concat_axis=1, tiled=True)  12.6 us
  transfers between devices with their start and end apart: 7, of which 6 were waited for; matrix products, arithmetic and copies ran while one was open for 10% of the time, Pallas kernels for 0%

commit v1 on v0

--- a/solution.py
+++ b/solution.py
@@ -75,7 +75,9 @@
     column_rows = lax.all_to_all(context, "shard", split_axis=1, concat_axis=0, tiled=True)
     row_count = out_weight.shape[0]
     piece_grad = lax.all_gather(grad_proj, "shard", axis=0, tiled=True)
-    piece_ids = lax.all_gather(modality, "shard", axis=0, tiled=True)
+    piece_ids = jnp.concatenate(
+        lax.all_to_all(jnp.stack([modality] * lax.axis_size("shard")), "shard", 0, 0), axis=0
+    )
     count = piece_grad.shape[0]
     piece_partial = jnp.zeros((count, row_count), jnp.float32)
     updated = []

time: 408 us -> 416 us (1.020)
  waiting for transfers between devices: 123 us -> 240 us
  blocking collectives: 145 us -> 31.5 us
  starting transfers between devices: 44.3 us -> 48.6 us
    all_gather x1 -> x0, blocking collectives: 113 us -> none  [local(): piece_ids = lax.all_gather(modality, 'shard', axis=0, tiled=True)]
    all_gather x1, waiting for transfers between devices: 0.02 us -> 106 us  [local(): piece_grad = lax.all_gather(grad_proj, 'shard', axis=0, tiled=True)]
    reduce_scatter x2, waiting for transfers between devices: 79.4 us -> 93.6 us  [sum_in_order(): pieces = lax.psum_scatter(pieces, axes[k], scatter_dimension=0, tiled=True)]
    all_to_all x0 -> x1, waiting for transfers between devices: none -> 10.2 us  [local(): lax.all_to_all(jnp.stack([modality] * lax.axis_size('shard')), 'shard', 0...]
    all_to_all x0 -> x1, starting transfers between devices: none -> 9.05 us  [local(): lax.all_to_all(jnp.stack([modality] * lax.axis_size('shard')), 'shard', 0...]
    all_to_all x1, waiting for transfers between devices: 15.5 us -> 8.62 us  [local(): lax.all_to_all(context, 'shard', split_axis=1, concat_axis=0, tiled=True)]
    all_to_all x1, waiting for transfers between devices: 6.73 us -> 0.01 us  [from_everyone(): lax.all_to_all(jnp.broadcast_to(shard[None], (count, *shard.shape)), axis...]
    all_to_all x1, starting transfers between devices: 10.1 us -> 5.43 us  [from_everyone(): lax.all_to_all(jnp.broadcast_to(shard[None], (count, *shard.shape)), axis...]
  transfers between devices with their start and end apart: 7 -> 8, of which waited for: 6 -> 7; matrix products, arithmetic and copies ran while one was open for 10% -> 10% of each run, Pallas kernels for 0% -> 0%
where the time goes in v1:
time: 416 us; the launch traced here: 415 us
  waiting for transfers between devices  240 us (58%)
  starting transfers between devices  48.6 us (12%)
  blocking collectives  31.5 us (8%)
  matrix products  28.9 us (7%)
  other arithmetic  27.8 us (7%)
  local copies, waits for them, and re-layouts  24.9 us (6%)
  between operations  13.9 us (3%)
    all_gather x1, waiting for transfers between devices, local(): piece_grad = lax.all_gather(grad_proj, 'shard', axis=0, tiled=True)  106 us
    reduce_scatter x2, waiting for transfers between devices, sum_in_order(): pieces = lax.psum_scatter(pieces, axes[k], scatter_dimension=0, tiled=True)  93.6 us
    all_to_all x1, blocking collectives, from_everyone(): lax.all_to_all(jnp.broadcast_to(shard[None], (count, *shard.shape)), axis...  31.5 us
    unnamed x1, other arithmetic  23.5 us
    all_to_all x1, starting transfers between devices, local(): lax.all_to_all(reduced, 'shard', split_axis=0, concat_axis=2, tiled=True)  15.1 us
    dot_general x3, matrix products, local(): lax.dot_general(masked, piece_grad, (((0,), (0,)), ((), ())), preferred_e...  14.8 us
    all_to_all x1, waiting for transfers between devices, local(): lax.all_to_all(spread, DP, split_axis=2, concat_axis=1, tiled=True)  12.6 us
    dot_general x3, matrix products, local(): lax.dot_general(piece_grad, out_weight[:, member, :], (((1,), (1,)), ((),...  11.4 us
  transfers between devices with their start and end apart: 8, of which 7 were waited for; matrix products, arithmetic and copies ran while one was open for 10% of the time, Pallas kernels for 0%

profile of v1, /device:TPU:32, one launch (start us, length us, event | category | flops | bytes accessed | tf_op | source)
XLA Modules:
  0.0 415.4 jit_solution(859353458539311078)
XLA Ops:
  7.9 1.4 fusion.16
  9.3 31.5 %all_to_all.69 = f32[8,1,256]{2,1,0:T(1,128)S(1)} all-to-all(f32[8,1,256]{2,1,0:T(1,128)S(1)} %broadcast_in_dim.32), channel_id=1, replica_groups=mesh['dp_0'=2,'dp_1'=4,'shard'=64] {'dp_0','dp_1'}, dimensions={0} | all-to-all | bytes 16384 | tf_op jit(solution)/shard_map/all_to_all | solution.py:14
  40.9 1.7 fusion.14
  42.6 1.3 stack.10
  43.9 9.0 %all-to-all-start = ((s32[64,1,128]{2,1,0:T(1,128)}), s32[64,1,128]{2,1,0:T(1,128)S(1)}, u32[]{:S(2)}, u32[]{:S(2)}) async-start(s32[64,1,128]{2,1,0:T(1,128)} %stack.10), calls=%async_computation | async-start | bytes 65536 | tf_op jit(solution)/shard_map/all_to_all | solution.py:79
  52.9 1.3 fusion.15
  54.2 10.2 %all-to-all-done = s32[64,1,128]{2,1,0:T(1,128)S(1)} async-done(((s32[64,1,128]{2,1,0:T(1,128)}), s32[64,1,128]{2,1,0:T(1,128)S(1)}, u32[]{:S(2)}, u32[]{:S(2)}) %all-to-all-start) | async-done | bytes 32800 | tf_op jit(solution)/shard_map/all_to_all | solution.py:79
  65.3 5.4 %all-to-all-start.5 = ((f32[64,3,512]{2,1,0:T(4,128)}), f32[64,3,512]{2,1,0:T(4,128)S(1)}, u32[]{:S(2)}, u32[]{:S(2)}) async-start(f32[64,3,512]{2,1,0:T(4,128)} %broadcast_in_dim.36), calls=%async_computation.7 | async-start | bytes 1048576 | tf_op jit(solution)/shard_map/all_to_all | solution.py:14
  70.8 106.1 %all-gather.2.cloned.1.call-done = bf16[8192,512]{1,0:T(8,128)(2,1)} async-done(((bf16[128,512]{1,0:T(8,128)(2,1)}), bf16[8192,512]{1,0:T(8,128)(2,1)}) %all-gather.2.cloned.1.call-update) | async-done | bytes 8388624 | tf_op jit(solution)/shard_map/all_gather | solution.py:77
  176.9 6.2 %convolution_multiply_fusion = f32[8192,64]{0,1:T(8,128)S(1)} fusion(bf16[8192,512]{1,0:T(8,128)(2,1)} %all-gather.2.cloned.1.call-done, f32[8192]{0:T(1024)S(1)} %get-tuple-element.11, bf16[64,3,512]{2,0,1:T(8,128)(2,1)} %param.10), kind=kOutput, calls=%fused_computation | convolution fusion | flops 537395200 | bytes 10584064 | tf_op jit(solution)/shard_map/dot_general | solution.py:86
  183.1 2.6 convolution_multiply_fusion.1
  185.7 2.6 fusion.1
  188.3 2.7 copy.46
  191.0 4.5 %copy.47 = f32[2,4,64,1,16,64]{5,4,2,0,1,3:T(8,128)} copy(f32[2,4,64,1,16,64]{5,4,1,0,2,3:T(8,128)} %bitcast.80) | data formatting | bytes 4194304 | tf_op jit(solution)/shard_map/reshape | solution.py:35
  195.6 1.2 copy-done.2
  196.8 1.3 copy.52
  198.1 9.1 %all-to-all-start.4 = ((bf16[128,64,64]{0,2,1:T(8,128)(2,1)}), bf16[128,64,64]{0,2,1:T(8,128)(2,1)S(1)}, u32[]{:S(2)}, u32[]{:S(2)}) async-start(bf16[128,64,64]{0,2,1:T(8,128)(2,1)} %bitcast.19), calls=%async_computation.6 | async-start | bytes 2097152 | tf_op jit(solution)/shard_map/all_to_all | solution.py:75
  207.2 40.2 %reduce-scatter.3.cloned.1.call-done = f32[2,64,1,16,64]{4,3,1,0,2:T(8,128)} async-done(((f32[8,64,1,16,64]{4,3,1,0,2:T(8,128)}), f32[2,64,1,16,64]{4,3,1,0,2:T(8,128)}) %reduce-scatter.3.cloned.1.call-update) | async-done | bytes 524304 | tf_op jit(solution)/shard_map/reduce_scatter | solution.py:39
  248.2 8.6 %all-to-all-done.4 = bf16[128,64,64]{0,2,1:T(8,128)(2,1)S(1)} async-done(((bf16[128,64,64]{0,2,1:T(8,128)(2,1)}), bf16[128,64,64]{0,2,1:T(8,128)(2,1)S(1)}, u32[]{:S(2)}, u32[]{:S(2)}) %all-to-all-start.4) | async-done | bytes 1048608 | tf_op jit(solution)/shard_map/all_to_all | solution.py:75
  256.8 4.9 %convolution_bitcast_fusion = f32[64,1,512]{2,0,1:T(8,128)S(1)} fusion(bf16[8192,512]{1,0:T(8,128)(2,1)} %all-gather.2.cloned.1.call-done, pred[8192]{0:T(1024)(128)(4,1)S(1)} %get-tuple-element.12, bf16[128,64,64]{0,2,1:T(8,128)(2,1)S(1)} %all-to-all-done.4), kind=kOutput, calls=%fused_computation.6 | convolution fusion | flops 537395200 | bytes 9576448 | tf_op jit(solution)/shard_map/dot_general | solution.py:95
  261.7 53.3 %reduce-scatter.5.cloned.1.call-done = f32[1,64,1,16,64]{4,3,1,0,2:T(8,128)} async-done(((f32[2,64,1,16,64]{4,3,1,0,2:T(8,128)}), f32[1,64,1,16,64]{4,3,1,0,2:T(8,128)}) %reduce-scatter.5.cloned.1.call-update) | async-done | bytes 262160 | tf_op jit(solution)/shard_map/reduce_scatter | solution.py:39
  317.0 15.1 %all-to-all-start.2 = ((bf16[64,2,512]{2,1,0:T(2,128)(2,1)}), bf16[64,2,512]{2,1,0:T(2,128)(2,1)S(1)}, u32[]{:S(2)}, u32[]{:S(2)}) async-start(bf16[64,2,512]{2,1,0:T(2,128)(2,1)} %reshape.100), calls=%async_computation.4 | async-start | bytes 262144 | tf_op jit(solution)/shard_map/all_to_all | solution.py:109
  332.1 4.9 %convolution_bitcast_fusion.1 = f32[64,1,512]{2,0,1:T(8,128)S(1)} fusion(bf16[8192,512]{1,0:T(8,128)(2,1)} %all-gather.2.cloned.1.call-done, pred[8192]{0:T(1024)(128)(4,1)S(1)} %get-tuple-element.14, bf16[128,64,64]{0,2,1:T(8,128)(2,1)S(1)} %all-to-all-done.4), kind=kOutput, calls=%fused_computation.7 | convolution fusion | flops 537395200 | bytes 9576448 | tf_op jit(solution)/shard_map/dot_general | solution.py:95
  337.0 8.7 %all-to-all-done.2 = bf16[64,2,512]{2,1,0:T(2,128)(2,1)S(1)} async-done(((bf16[64,2,512]{2,1,0:T(2,128)(2,1)}), bf16[64,2,512]{2,1,0:T(2,128)(2,1)S(1)}, u32[]{:S(2)}, u32[]{:S(2)}) %all-to-all-start.2) | async-done | bytes 131104 | tf_op jit(solution)/shard_map/all_to_all | solution.py:109
  346.3 2.7 copy.49
  349.6 23.5 %reduce.1 = bf16[4096,16]{1,0:T(8,128)(2,1)} reduce(bf16[4096,1,16]{2,1,0:T(2,128)(2,1)S(1)} %bitcast.81, bf16[]{:T(256)} %broadcast.70), dimensions={1}, to_apply=%bitcast.57.reduce_sub_computation | reduce | bytes 262146
  373.0 3.1 reshape.102
  376.1 9.9 %all-to-all-start.3 = ((bf16[8,2,4096]{2,1,0:T(2,128)(2,1)}), bf16[8,2,4096]{2,1,0:T(2,128)(2,1)S(1)}, u32[]{:S(2)}, u32[]{:S(2)}) async-start(bf16[8,2,4096]{2,1,0:T(2,128)(2,1)} %reshape.102), calls=%async_computation.5 | async-start | bytes 262144 | tf_op jit(solution)/shard_map/all_to_all | solution.py:110
  386.0 4.9 %convolution_bitcast_fusion.2 = f32[64,1,512]{2,0,1:T(8,128)S(1)} fusion(bf16[8192,512]{1,0:T(8,128)(2,1)} %all-gather.2.cloned.1.call-done, pred[8192]{0:T(1024)(128)(4,1)S(1)} %get-tuple-element.6, bf16[128,64,64]{0,2,1:T(8,128)(2,1)S(1)} %all-to-all-done.4), kind=kOutput, calls=%fused_computation.8 | convolution fusion | flops 537395200 | bytes 9576448 | tf_op jit(solution)/shard_map/dot_general | solution.py:95
  391.7 12.6 %all-to-all-done.3 = bf16[8,2,4096]{2,1,0:T(2,128)(2,1)S(1)} async-done(((bf16[8,2,4096]{2,1,0:T(2,128)(2,1)}), bf16[8,2,4096]{2,1,0:T(2,128)(2,1)S(1)}, u32[]{:S(2)}, u32[]{:S(2)}) %all-to-all-start.3) | async-done | bytes 131104 | tf_op jit(solution)/shard_map/all_to_all | solution.py:110
  404.3 1.8 reshape.103
  406.1 2.0 copy.50
  (31 shorter events, 7.0 us)
Async XLA Ops:
  7.2 0.7 copy-start
  7.2 169.7 %all-gather.2.cloned.1.call-start = ((), (), s32[]{:S(2)}) async-start(), calls=%async_computation.8 | async-start | bytes 8519680 | tf_op jit(solution)/shard_map/all_gather | solution.py:77
  43.9 20.5 %all-to-all-start = ((s32[64,1,128]{2,1,0:T(1,128)}), s32[64,1,128]{2,1,0:T(1,128)S(1)}, u32[]{:S(2)}, u32[]{:S(2)}) async-start(s32[64,1,128]{2,1,0:T(1,128)} %stack.10), calls=%async_computation | async-start | bytes 65536 | tf_op jit(solution)/shard_map/all_to_all | solution.py:79
  65.3 132.8 %all-to-all-start.5 = ((f32[64,3,512]{2,1,0:T(4,128)}), f32[64,3,512]{2,1,0:T(4,128)S(1)}, u32[]{:S(2)}, u32[]{:S(2)}) async-start(f32[64,3,512]{2,1,0:T(4,128)} %broadcast_in_dim.36), calls=%async_computation.7 | async-start | bytes 1048576 | tf_op jit(solution)/shard_map/all_to_all | solution.py:14
  70.7 176.7 %reduce-scatter.3.cloned.1.call-start = ((), (), s32[]{:S(2)}) async-start(), calls=%async_computation.9 | async-start | bytes 5242880 | tf_op jit(solution)/shard_map/reduce_scatter | solution.py:39
  176.9 6.2 %copy-start.1 = (bf16[8192,512]{1,0:T(8,128)(2,1)S(1)}, bf16[8192,512]{1,0:T(8,128)(2,1)}, u32[]{:S(2)}) copy-start(bf16[8192,512]{1,0:T(8,128)(2,1)} %all-gather.2.cloned.1.call-done) | copy-start | bytes 25165828
  176.9 6.2 %copy-start.3 = (bf16[64,3,512]{2,0,1:T(8,128)(2,1)S(1)}, bf16[64,3,512]{2,0,1:T(8,128)(2,1)}, u32[]{:S(2)}) copy-start(bf16[64,3,512]{2,0,1:T(8,128)(2,1)} %param.10) | copy-start | bytes 589828
  195.6 1.2 copy-start.2
  198.1 58.7 %all-to-all-start.4 = ((bf16[128,64,64]{0,2,1:T(8,128)(2,1)}), bf16[128,64,64]{0,2,1:T(8,128)(2,1)S(1)}, u32[]{:S(2)}, u32[]{:S(2)}) async-start(bf16[128,64,64]{0,2,1:T(8,128)(2,1)} %bitcast.19), calls=%async_computation.6 | async-start | bytes 2097152 | tf_op jit(solution)/shard_map/all_to_all | solution.py:75
  207.2 107.9 %reduce-scatter.5.cloned.1.call-start = ((), (), s32[]{:S(2)}) async-start(), calls=%async_computation.10 | async-start | bytes 1572864 | tf_op jit(solution)/shard_map/reduce_scatter | solution.py:39
  317.0 28.7 %all-to-all-start.2 = ((bf16[64,2,512]{2,1,0:T(2,128)(2,1)}), bf16[64,2,512]{2,1,0:T(2,128)(2,1)S(1)}, u32[]{:S(2)}, u32[]{:S(2)}) async-start(bf16[64,2,512]{2,1,0:T(2,128)(2,1)} %reshape.100), calls=%async_computation.4 | async-start | bytes 262144 | tf_op jit(solution)/shard_map/all_to_all | solution.py:109
  376.1 28.2 %all-to-all-start.3 = ((bf16[8,2,4096]{2,1,0:T(2,128)(2,1)}), bf16[8,2,4096]{2,1,0:T(2,128)(2,1)S(1)}, u32[]{:S(2)}, u32[]{:S(2)}) async-start(bf16[8,2,4096]{2,1,0:T(2,128)(2,1)} %reshape.102), calls=%async_computation.5 | async-start | bytes 262144 | tf_op jit(solution)/shard_map/all_to_all | solution.py:110
Sparse Core Ops, SparseCore 0:
  42.7 134.1 all-gather.1
  195.7 51.6 reduce-scatter.2
  250.3 64.7 reduce-scatter.4
